TPU v7x, 512 devices: a whole 4x8x8 slice. The times are simulated.
512 devices in a mesh: pipe: 8 (over y_hi, core), ctx: 16 (over z, y_lo), dp: 4 (over x).
Axes of the slice: x: 4, y: 8 (y_hi: 4, y_lo: 2; y = y_hi * 2 + y_lo), z: 8, core: 2. Of those that a mesh axis runs over, the one named last changes fastest.
Arguments:
- state: bfloat16 [8, 4, 2048, 1024], P('pipe', 'dp', 'ctx'), may hold values from -36 to 36
- weights: bfloat16 [2, 8, 1024, 256], P(None, 'pipe'), may hold values from -0.1875 to 0.1875
- out_grad: bfloat16 [2, 8, 4, 2048, 1024], P(None, 'pipe', 'dp', 'ctx'), may hold values from -0.59765625 to 0.59765625
- start_span: int32 [8, 4], P(None, 'dp'), may hold values from 0 to 1
- block_order: int32 [32], replicated, may hold values from 0 to 31, each once
Outputs:
- state_out: bfloat16 [8, 4, 2048, 1024], P('pipe', 'dp', 'ctx')
- weight_grads: float32 [2, 8, 1024, 256], P(None, 'pipe')
All inputs are finite; a program needn't handle non-finite values.
Results may differ from a plain program's by a relative error of at most 0.012.
Values may be sent and summed in bfloat16 or wider, within the bound.
No kernel may reach another device: no remote copies, remote signals or barrier semaphores. Data moves between devices by JAX's collectives and lax.ppermute only.
A program may use at most 64 MiB of HBM per device.

v0:
```python
import math
import jax
import jax.numpy as jnp
from jax import lax
from jax.sharding import PartitionSpec as P

EPS = 1e-05


def from_behind(block, axis, distance):
    devices = range(lax.axis_size(axis))
    route = [((i - distance) % len(devices), i) for i in devices]
    return lax.ppermute(block, axis, route)


def rms_scale(values):
    return lax.rsqrt(jnp.mean(values * values, axis=-1, keepdims=True) + EPS)


def token_positions(block_order, seq_total):
    half_count = block_order.shape[0]
    half_len = seq_total // half_count
    row_ids = jnp.arange(seq_total, dtype=jnp.int32)
    selected = (row_ids // half_len)[:, None] == jnp.arange(half_count, dtype=jnp.int32)[None, :]
    block_ids = jnp.sum(jnp.where(selected, block_order[None, :], 0), axis=1)
    return block_ids * half_len + row_ids % half_len


def shards(state, weights, out_grad, start_span, block_order):
    tok_rows = state.shape[2]
    feat_width = state.shape[3]
    head_dim = weights.shape[3] // 2
    head_count = feat_width // head_dim
    group_size = math.gcd(head_count, 4)
    group_count = head_count // group_size
    span_count = weights.shape[0]
    section_count = lax.axis_size("pipe")
    seq_total = tok_rows * lax.axis_size("ctx")
    score_scale = 1.0 / math.sqrt(head_dim)
    all_positions = token_positions(block_order, seq_total)
    own_positions = lax.dynamic_slice_in_dim(
        all_positions, lax.axis_index("ctx") * tok_rows, tok_rows
    )
    causal = all_positions[None, :] <= own_positions[:, None]
    section_index = lax.axis_index("pipe")
    carried = state[0, 0]
    start_column = start_span[:, 0]
    weight_grads = jnp.zeros((span_count, feat_width, 2 * head_dim), jnp.float32)
    for tick_index in range(out_grad.shape[0]):
        anchor = (section_index - tick_index) % section_count
        first_span = jnp.sum(
            jnp.where(jnp.arange(section_count, dtype=jnp.int32) == anchor, start_column, 0)
        )
        span_index = (first_span + (anchor + tick_index) // section_count) % 2
        weight = lax.dynamic_index_in_dim(weights[:, 0], span_index, 0, keepdims=False)
        widened = carried.astype(jnp.float32)
        normed = (widened * rms_scale(widened)).astype(jnp.bfloat16)
        split_heads = widened.reshape(tok_rows, head_count, head_dim)
        queries = (split_heads * rms_scale(split_heads)).astype(jnp.bfloat16)
        projected = jnp.dot(normed, weight, preferred_element_type=jnp.float32)
        key_raw = projected[:, :head_dim]
        key_scale = rms_scale(key_raw)
        key_unit = key_raw * key_scale
        own_rows = jnp.concatenate([key_unit, projected[:, head_dim:]], axis=1).astype(jnp.bfloat16)
        gathered = lax.all_gather(own_rows, "ctx", axis=0, tiled=True)
        key_rows = gathered[:, :head_dim]
        value_rows = gathered[:, head_dim:]
        query_groups = queries.reshape(tok_rows, group_count, group_size, head_dim).transpose(
            1, 0, 2, 3
        )

        def forward_group(query_part):
            scores = (
                jnp.einsum("qhd,kd->hqk", query_part, key_rows, preferred_element_type=jnp.float32)
                * score_scale
            )
            exponent = jnp.where(causal[None], jnp.exp(scores), 0.0)
            total_weight = jnp.sum(exponent, axis=-1, keepdims=True)
            probs = (exponent / total_weight).astype(jnp.bfloat16)
            attended = jnp.einsum(
                "hqk,kd->qhd", probs, value_rows, preferred_element_type=jnp.float32
            )
            return (probs, attended)

        probs, attended = lax.map(forward_group, query_groups)
        output = attended.transpose(1, 0, 2, 3).reshape(tok_rows, feat_width)
        updated = (widened + output * rms_scale(output)).astype(jnp.bfloat16)
        carried = from_behind(updated, "pipe", 1)
        upstream = out_grad[tick_index, 0, 0]
        upstream_groups = upstream.reshape(tok_rows, group_count, group_size, head_dim).transpose(
            1, 0, 2, 3
        )
        row_delta = jnp.sum(upstream_groups.astype(jnp.float32) * attended, axis=-1).transpose(
            0, 2, 1
        )
        key_grad = jnp.zeros((tok_rows * lax.axis_size("ctx"), head_dim), jnp.float32)
        value_grad = jnp.zeros((tok_rows * lax.axis_size("ctx"), head_dim), jnp.float32)
        for head_block in range(group_count):
            prob_part = probs[head_block]
            value_grad = value_grad + jnp.einsum(
                "hqk,qhd->kd",
                prob_part,
                upstream_groups[head_block],
                preferred_element_type=jnp.float32,
            )
            prob_grad = jnp.einsum(
                "qhd,kd->hqk",
                upstream_groups[head_block],
                value_rows,
                preferred_element_type=jnp.float32,
            )
            score_grad = (
                prob_part.astype(jnp.float32)
                * (prob_grad - row_delta[head_block][..., None])
                * score_scale
            ).astype(jnp.bfloat16)
            key_grad = key_grad + jnp.einsum(
                "hqk,qhd->kd",
                score_grad,
                query_groups[head_block],
                preferred_element_type=jnp.float32,
            )
        key_sums = lax.psum_scatter(
            jnp.concatenate([key_grad, value_grad], axis=1).astype(jnp.bfloat16),
            "ctx",
            scatter_dimension=0,
            tiled=True,
        ).astype(jnp.float32)
        key_delta = key_sums[:, :head_dim]
        key_back = key_scale * (
            key_delta - key_unit * jnp.mean(key_delta * key_unit, axis=-1, keepdims=True)
        )
        grad_rows = jnp.concatenate([key_back, key_sums[:, head_dim:]], axis=1).astype(jnp.bfloat16)
        local_grad = lax.dot_general(
            normed, grad_rows, (((0,), (0,)), ((), ())), preferred_element_type=jnp.float32
        )
        span_mask = (jnp.arange(span_count, dtype=jnp.int32) == span_index).astype(jnp.float32)[
            :, None, None
        ]
        masked_grad = span_mask * local_grad
        weight_grads = weight_grads + masked_grad
    weight_grads = lax.psum(weight_grads, ("ctx", "dp"))
    return (carried[None, None], weight_grads[:, None])


def solution(mesh):
    return jax.shard_map(
        shards,
        mesh=mesh,
        in_specs=(
            P("pipe", "dp", "ctx", None),
            P(None, "pipe", None, None),
            P(None, "pipe", "dp", "ctx", None),
            P(None, "dp"),
            P(),
        ),
        out_specs=(P("pipe", "dp", "ctx", None), P(None, "pipe", None, None)),
        check_vma=False,
    )
```

profile of v0, /device:TPU:16, one launch (start us, length us, event | category | flops | bytes accessed | tf_op | source)
XLA Modules:
  0.0 990.2 jit_solution(8186478735265335391)
XLA Ops:
  7.3 1.4 fusion.99
  10.5 1.2 fusion.58
  16.2 74.4 %all-gather.3.cloned.1.call-done = bf16[2048,256]{1,0:T(8,128)(2,1)} async-done(((bf16[128,256]{1,0:T(8,128)(2,1)}), bf16[2048,256]{1,0:T(8,128)(2,1)}) %all-gather.3.cloned.1.call-update) | async-done | bytes 1048592 | tf_op jit(solution)/shard_map/all_gather | solution.py:65
  90.6 1.3 fusion.117
  92.7 2.5 broadcast.232.clone2
  95.2 22.0 %while.26 = (s32[]{:T(128)}, bf16[2,4,128,2048]{2,3,1,0:T(8,128)(2,1)}, f32[2,128,4,128]{3,1,2,0:T(8,128)}, bf16[2,128,4,128]{1,3,2,0:T(8,128)(2,1)}, bf16[2048,...) while((s32[]{:T(128)}, ...), condition=%wide.region_7.8_spmd.clone, body=%wide.region_5.7_spmd.clone.sunk | while | flops 548666880 | bytes 33962720 | solution.py:85
  95.4 2.3 bitcast_reduce_fusion.4
  97.8 1.8 fusion.136
  100.5 2.5 copy.225
  103.0 3.2 constant_dynamic-update-slice_fusion.4
  106.4 2.3 bitcast_reduce_fusion.4
  108.8 1.8 fusion.136
  111.5 2.5 copy.225
  114.0 3.1 constant_dynamic-update-slice_fusion.4
  118.4 1.4 copy.152
  120.1 1.9 collective-permute-start
  122.8 6.8 collective-permute-done
  132.6 1.3 multiply_reduce_fusion.1
  134.4 2.3 convolution_bitcast_fusion.6
  136.7 2.3 fusion.38
  139.0 4.0 convolution_bitcast_fusion.8
  143.1 3.4 fusion.39
  149.1 56.5 %all-gather.5.cloned.1.call-done = bf16[2048,256]{1,0:T(8,128)(2,1)} async-done(((bf16[128,256]{1,0:T(8,128)(2,1)}), bf16[2048,256]{1,0:T(8,128)(2,1)}) %all-gather.5.cloned.1.call-update) | async-done | bytes 1048592 | tf_op jit(solution)/shard_map/all_gather | solution.py:65
  205.6 1.3 fusion.116
  207.7 2.5 broadcast.232.clone
  210.1 22.0 %while.27 = (s32[]{:T(128)}, bf16[2,4,128,2048]{2,3,1,0:T(8,128)(2,1)}, f32[2,128,4,128]{3,1,2,0:T(8,128)}, bf16[2,128,4,128]{1,3,2,0:T(8,128)(2,1)}, bf16[2048,...) while((s32[]{:T(128)}, ...), condition=%wide.region_15.16_spmd.clone, body=%wide.region_13.15_spmd.clone.sunk | while | flops 548666880 | bytes 33962720 | solution.py:85
  210.4 2.3 bitcast_reduce_fusion.5
  212.7 1.8 fusion.140
  215.5 2.5 copy.226
  218.0 3.2 constant_dynamic-update-slice_fusion.5
  221.4 2.3 bitcast_reduce_fusion.5
  223.7 1.8 fusion.140
  226.5 2.5 copy.226
  229.0 3.1 constant_dynamic-update-slice_fusion.5
  232.1 1.4 multiply_reduce_fusion
  233.6 2.3 convolution_bitcast_fusion.2
  235.9 2.3 fusion.36
  238.2 3.9 convolution_bitcast_fusion.4
  242.1 4.0 fusion.37
  246.2 2.2 pad_maximum_fusion.1
  248.4 35.8 %reduce-scatter.3.cloned.1.call-done = bf16[128,256]{1,0:T(8,128)(2,1)} async-done(((bf16[2048,256]{1,0:T(8,128)(2,1)}), bf16[128,256]{1,0:T(8,128)(2,1)}) %reduce-scatter.3.cloned.1.call-update) | async-done | bytes 65552 | tf_op jit(solution)/shard_map/reduce_scatter | solution.py:123
  287.2 73.8 %reduce-scatter.5.cloned.1.call-done = bf16[128,256]{1,0:T(8,128)(2,1)} async-done(((bf16[2048,256]{1,0:T(8,128)(2,1)}), bf16[128,256]{1,0:T(8,128)(2,1)}) %reduce-scatter.5.cloned.1.call-update) | async-done | bytes 65552 | tf_op jit(solution)/shard_map/reduce_scatter | solution.py:123
  363.9 1.7 add_bitcast_fusion
  365.6 1.4 copy.156
  368.5 1.9 collective-permute-start.1
  370.5 7.2 collective-permute-done.1
  377.7 602.2 %all-reduce.2.cloned.1.call-done = f32[2,1,1024,256]{3,2,1,0:T(8,128)} async-done(((f32[2,1,1024,256]{3,2,1,0:T(8,128)}), f32[2,1,1024,256]{3,2,1,0:T(8,128)}) %all-reduce.2.cloned.1.call-update) | async-done | bytes 2097168 | tf_op jit(solution)/shard_map/psum | solution.py:142
  980.6 3.0 copy.256
  (144 shorter events, 27.6 us)
Async XLA Ops:
  7.2 3.3 copy-start
  7.2 8.0 copy-start.23
  7.2 83.4 %all-gather.3.cloned.1.call-start = ((), (), s32[]{:S(2)}) async-start(), calls=%async_computation.2 | async-start | bytes 1114112 | tf_op jit(solution)/shard_map/all_gather | solution.py:65
  10.5 1.4 copy-start.19
  12.6 192.9 %all-gather.5.cloned.1.call-start = ((), (), s32[]{:S(2)}) async-start(), calls=%async_computation.3 | async-start | bytes 1114112 | tf_op jit(solution)/shard_map/all_gather | solution.py:65
  95.2 24.8 %copy-start.1 = (bf16[1,1,128,1024]{3,2,1,0:T(8,128)(2,1)S(1)}, bf16[1,1,128,1024]{3,2,1,0:T(8,128)(2,1)}, u32[]{:S(2)}) copy-start(bf16[1,1,128,1024]{3,2,1,0:T(8,128)(2,1)} %param.9) | copy-start | bytes 786436
  95.2 2.6 copy-start.13
  95.2 2.6 copy-start.15
  103.0 3.2 copy-start.14
  103.0 3.2 copy-start.16
  106.2 2.6 copy-start.13
  106.2 2.6 copy-start.15
  114.0 3.1 copy-start.14
  114.0 3.1 copy-start.16
  117.1 14.0 %copy-start.8 = (bf16[2,1,1,128,1024]{4,3,2,1,0:T(8,128)(2,1)S(1)}, bf16[2,1,1,128,1024]{4,3,2,1,0:T(8,128)(2,1)}, u32[]{:S(2)}) copy-start(bf16[2,1,1,128,1024]{4,3,2,1,0:T(8,128)(2,1)} %param.11) | copy-start | bytes 1572868
  120.1 9.4 collective-permute-start
  129.6 18.6 %copy-start.2 = (bf16[128,1024]{1,0:T(8,128)(2,1)}, bf16[128,1024]{1,0:T(8,128)(2,1)S(1)}, u32[]{:S(2)}) copy-start(bf16[128,1024]{1,0:T(8,128)(2,1)S(1)} %collective-permute-done) | copy-start | bytes 786436
  129.7 0.6 copy-start.21
  130.0 4.4 copy-start.5
  130.3 0.9 copy-start.17
  131.1 153.1 %reduce-scatter.3.cloned.1.call-start = ((), (), s32[]{:S(2)}) async-start(), calls=%async_computation.4 | async-start | bytes 1114112 | tf_op jit(solution)/shard_map/reduce_scatter | solution.py:123
  147.6 213.4 %reduce-scatter.5.cloned.1.call-start = ((), (), s32[]{:S(2)}) async-start(), calls=%async_computation.5 | async-start | bytes 1114112 | tf_op jit(solution)/shard_map/reduce_scatter | solution.py:123
  210.1 2.6 copy-start.9
  210.1 2.6 copy-start.11
  218.0 3.2 copy-start.10
  218.0 3.2 copy-start.12
  221.2 2.6 copy-start.9
  221.2 2.6 copy-start.11
  229.0 3.1 copy-start.10
  229.0 3.1 copy-start.12
  232.1 3.8 copy-start.4
  232.1 6.1 copy-start.7
  242.1 44.6 %copy-start.20 = (f32[128]{0:T(128)S(1)}, f32[128]{0:T(128)}, u32[]{:S(2)}) copy-start(f32[128]{0:T(128)} %copy-done.19) | copy-start | bytes 1540
  246.1 114.8 %copy-start.6 = (f32[128,256]{1,0:T(8,128)S(1)}, f32[128,256]{1,0:T(8,128)}, u32[]{:S(2)}) copy-start(f32[128,256]{1,0:T(8,128)} %copy-done.5) | copy-start | bytes 393220
  246.1 114.8 %copy-start.18 = (f32[128]{0:T(128)S(1)}, f32[128]{0:T(128)}, u32[]{:S(2)}) copy-start(f32[128]{0:T(128)} %copy-done.17) | copy-start | bytes 1540
  246.1 117.4 %copy-start.3 = (bf16[128,1024]{1,0:T(8,128)(2,1)S(1)}, bf16[128,1024]{1,0:T(8,128)(2,1)}, u32[]{:S(2)}) copy-start(bf16[128,1024]{1,0:T(8,128)(2,1)} %copy-done.2) | copy-start | bytes 786436
  246.1 117.4 %copy-start.22 = (f32[128]{0:T(128)S(1)}, f32[128]{0:T(128)}, u32[]{:S(2)}) copy-start(f32[128]{0:T(128)} %copy-done.21) | copy-start | bytes 1540
  248.4 731.6 %all-reduce.2.cloned.1.call-start = ((), (), s32[]{:S(2)}) async-start(), calls=%async_computation.6 | async-start | bytes 4194304 | tf_op jit(solution)/shard_map/psum | solution.py:142
  368.5 9.2 collective-permute-start.1
Sparse Core Ops, SparseCore 0:
  12.8 77.7 all-gather.2
  131.2 74.3 all-gather.4
  208.4 75.7 reduce-scatter.2
  287.7 73.2 reduce-scatter.4
  365.7 614.1 all-reduce.1
where the time goes:
time: 992 us; the launch traced here: 990 us
  waiting for transfers between devices  857 us (86%)
  local copies, waits for them, and re-layouts  44.1 us (4%)
  matrix products  43.5 us (4%)
  other arithmetic  25.8 us (3%)
  between operations  15.7 us (2%)
    psum x1, waiting for transfers between devices, shards(): weight_grads = lax.psum(weight_grads, ('ctx', 'dp'))  602 us
    all_gather x2, waiting for transfers between devices, shards(): gathered = lax.all_gather(own_rows, 'ctx', axis=0, tiled=True)  131 us
    reduce_scatter x2, waiting for transfers between devices, shards(): lax.psum_scatter(jnp.concatenate([key_grad, value_grad], axis=1).astype(j...  110 us
    dynamic_update_slice x8, local copies, waits for them, and re-layouts, shards(): probs, attended = lax.map(forward_group, query_groups)  22.5 us
  transfers between devices with their start and end apart: 7, of which 7 were waited for; matrix products, arithmetic and copies ran while one was open for 7% of the time, Pallas kernels for 0%

commit v1 on v0

--- a/solution.py
+++ b/solution.py
@@ -3,6 +3,7 @@
 import jax.numpy as jnp
 from jax import lax
 from jax.sharding import PartitionSpec as P
+from jax.lax import psum
 
 EPS = 1e-05
 
@@ -139,7 +140,10 @@
         ]
         masked_grad = span_mask * local_grad
         weight_grads = weight_grads + masked_grad
-    weight_grads = lax.psum(weight_grads, ("ctx", "dp"))
+    inputs = weight_grads
+    for it in ("ctx", "dp"):
+        inputs = psum(inputs, it)
+    weight_grads = inputs
     return (carried[None, None], weight_grads[:, None])
 
 

time: 992 us -> 603 us (0.61)
  the two profiles are of different devices: /device:TPU:16 before, /device:TPU:1 now
where the time goes in v1:
time: 603 us; the launch traced here: 602 us
  waiting for transfers between devices  444 us (74%)
  local copies, waits for them, and re-layouts  44.1 us (7%)
  matrix products  43.5 us (7%)
  starting transfers between devices  28.5 us (5%)
  other arithmetic  25.8 us (4%)
  between operations  16 us (3%)
    psum x2, waiting for transfers between devices, shards(): inputs = psum(inputs, it)  213 us
    all_gather x2, waiting for transfers between devices, shards(): gathered = lax.all_gather(own_rows, 'ctx', axis=0, tiled=True)  114 us
    reduce_scatter x2, waiting for transfers between devices, shards(): lax.psum_scatter(jnp.concatenate([key_grad, value_grad], axis=1).astype(j...  108 us
    ppermute x2, starting transfers between devices, from_behind(): return lax.ppermute(block, axis, route)  28.1 us
    dynamic_update_slice x8, local copies, waits for them, and re-layouts, shards(): probs, attended = lax.map(forward_group, query_groups)  22.5 us
    dot_general x4, matrix products, shards(): jnp.einsum('hqk,qhd->kd', score_grad, query_groups[head_block], preferred...  15.3 us
  transfers between devices with their start and end apart: 8, of which 8 were waited for; matrix products, arithmetic and copies ran while one was open for 12% of the time, Pallas kernels for 0%

profile of v1, /device:TPU:1, one launch (start us, length us, event | category | flops | bytes accessed | tf_op | source)
XLA Modules:
  0.0 602.1 jit_solution(10659373649664996307)
XLA Ops:
  7.3 1.4 fusion.99
  16.2 65.9 %all-gather.3.cloned.1.call-done = bf16[2048,256]{1,0:T(8,128)(2,1)} async-done(((bf16[128,256]{1,0:T(8,128)(2,1)}), bf16[2048,256]{1,0:T(8,128)(2,1)}) %all-gather.3.cloned.1.call-update) | async-done | bytes 1048592 | tf_op jit(solution)/shard_map/all_gather | solution.py:66
  82.1 1.3 fusion.117
  84.2 2.5 broadcast.232.clone2
  86.7 22.0 %while.26 = (s32[]{:T(128)}, bf16[2,4,128,2048]{2,3,1,0:T(8,128)(2,1)}, f32[2,128,4,128]{3,1,2,0:T(8,128)}, bf16[2,128,4,128]{1,3,2,0:T(8,128)(2,1)}, bf16[2048,...) while((s32[]{:T(128)}, ...), condition=%wide.region_7.8_spmd.clone, body=%wide.region_5.7_spmd.clone.sunk | while | flops 548666880 | bytes 33962720 | solution.py:86
  86.9 2.3 bitcast_reduce_fusion.4
  89.3 1.8 fusion.136
  92.0 2.5 copy.225
  94.5 3.2 constant_dynamic-update-slice_fusion.4
  97.9 2.3 bitcast_reduce_fusion.4
  100.3 1.8 fusion.136
  103.0 2.5 copy.225
  105.5 3.1 constant_dynamic-update-slice_fusion.4
  109.9 1.4 copy.152
  111.6 14.1 %collective-permute-start = (bf16[128,1024]{1,0:T(8,128)(2,1)S(1)}, bf16[128,1024]{1,0:T(8,128)(2,1)S(1)}, u32[]{:S(2)}, u32[]{:S(2)}) collective-permute-start(bf16[128,1024]{1,0:T(8,128)(2,1)S(1)} %fusion.63), channel_id=1, source_target_pairs={{448,0},{0,64},{64,128},{128,192},{192,256},{256,320},{320,384},{3... | collective-permute-start | bytes 786440 | tf_op jit(solution)/shard_map/ppermute | solution.py:14
  126.5 2.7 collective-permute-done
  132.2 1.3 multiply_reduce_fusion.1
  134.0 2.3 convolution_bitcast_fusion.6
  136.3 2.3 fusion.38
  138.6 4.0 convolution_bitcast_fusion.8
  142.6 3.4 fusion.39
  148.6 48.4 %all-gather.5.cloned.1.call-done = bf16[2048,256]{1,0:T(8,128)(2,1)} async-done(((bf16[128,256]{1,0:T(8,128)(2,1)}), bf16[2048,256]{1,0:T(8,128)(2,1)}) %all-gather.5.cloned.1.call-update) | async-done | bytes 1048592 | tf_op jit(solution)/shard_map/all_gather | solution.py:66
  197.1 1.3 fusion.116
  199.2 2.5 broadcast.232.clone
  201.6 21.9 %while.27 = (s32[]{:T(128)}, bf16[2,4,128,2048]{2,3,1,0:T(8,128)(2,1)}, f32[2,128,4,128]{3,1,2,0:T(8,128)}, bf16[2,128,4,128]{1,3,2,0:T(8,128)(2,1)}, bf16[2048,...) while((s32[]{:T(128)}, ...), condition=%wide.region_15.16_spmd.clone, body=%wide.region_13.15_spmd.clone.sunk | while | flops 548666880 | bytes 33962720 | solution.py:86
  201.9 2.3 bitcast_reduce_fusion.5
  204.2 1.8 fusion.140
  207.0 2.5 copy.226
  209.5 3.2 constant_dynamic-update-slice_fusion.5
  212.9 2.3 bitcast_reduce_fusion.5
  215.2 1.8 fusion.140
  218.0 2.5 copy.226
  220.5 3.1 constant_dynamic-update-slice_fusion.5
  223.6 1.4 multiply_reduce_fusion
  225.0 2.3 convolution_bitcast_fusion.2
  227.3 2.3 fusion.36
  229.7 3.9 convolution_bitcast_fusion.4
  233.6 4.0 fusion.37
  237.6 2.2 pad_maximum_fusion.1
  239.9 34.3 %reduce-scatter.3.cloned.1.call-done = bf16[128,256]{1,0:T(8,128)(2,1)} async-done(((bf16[2048,256]{1,0:T(8,128)(2,1)}), bf16[128,256]{1,0:T(8,128)(2,1)}) %reduce-scatter.3.cloned.1.call-update) | async-done | bytes 65552 | tf_op jit(solution)/shard_map/reduce_scatter | solution.py:124
  277.1 73.9 %reduce-scatter.5.cloned.1.call-done = bf16[128,256]{1,0:T(8,128)(2,1)} async-done(((bf16[2048,256]{1,0:T(8,128)(2,1)}), bf16[128,256]{1,0:T(8,128)(2,1)}) %reduce-scatter.5.cloned.1.call-update) | async-done | bytes 65552 | tf_op jit(solution)/shard_map/reduce_scatter | solution.py:124
  354.0 1.7 multiply_add_fusion
  355.8 157.4 %all-reduce.3.cloned.1.call-done = f32[2,1024,256]{2,1,0:T(8,128)} async-done(((f32[2,1024,256]{2,1,0:T(8,128)}), f32[2,1024,256]{2,1,0:T(8,128)}) %all-reduce.3.cloned.1.call-update) | async-done | bytes 2097168 | tf_op jit(solution)/shard_map/psum | solution.py:145
  513.2 1.4 copy.156
  516.1 14.0 %collective-permute-start.1 = (bf16[128,1024]{1,0:T(8,128)(2,1)S(1)}, bf16[128,1024]{1,0:T(8,128)(2,1)S(1)}, u32[]{:S(2)}, u32[]{:S(2)}) collective-permute-start(bf16[128,1024]{1,0:T(8,128)(2,1)S(1)} %add_convert_fusion), channel_id=1, source_target_pairs={{448,0},{0,64},{64,128},{128,192},{192,256},{256,320},{320,384},{3... | collective-permute-start | bytes 786440 | tf_op jit(solution)/shard_map/ppermute | solution.py:14
  530.1 5.7 collective-permute-done.1
  535.8 55.7 %all-reduce.5.cloned.1.call-done = f32[2,1,1024,256]{3,2,1,0:T(8,128)} async-done(((f32[2,1,1024,256]{3,2,1,0:T(8,128)}), f32[2,1,1024,256]{3,2,1,0:T(8,128)}) %all-reduce.5.cloned.1.call-update) | async-done | bytes 2097168 | tf_op jit(solution)/shard_map/psum | solution.py:145
  592.2 3.0 copy.257
  (147 shorter events, 28.9 us)
Async XLA Ops:
  7.2 3.3 copy-start
  7.2 8.0 %copy-start.23 = (s32[32]{0:T(128)S(1)}, s32[32]{0:T(128)}, u32[]{:S(2)}) copy-start(s32[32]{0:T(128)} %param.13) | copy-start | bytes 388
  7.2 74.9 %all-gather.3.cloned.1.call-start = ((), (), s32[]{:S(2)}) async-start(), calls=%async_computation.2 | async-start | bytes 1114112 | tf_op jit(solution)/shard_map/all_gather | solution.py:66
  10.5 1.4 copy-start.19
  12.6 184.4 %all-gather.5.cloned.1.call-start = ((), (), s32[]{:S(2)}) async-start(), calls=%async_computation.3 | async-start | bytes 1114112 | tf_op jit(solution)/shard_map/all_gather | solution.py:66
  86.7 24.8 %copy-start.1 = (bf16[1,1,128,1024]{3,2,1,0:T(8,128)(2,1)S(1)}, bf16[1,1,128,1024]{3,2,1,0:T(8,128)(2,1)}, u32[]{:S(2)}) copy-start(bf16[1,1,128,1024]{3,2,1,0:T(8,128)(2,1)} %param.9) | copy-start | bytes 786436
  86.7 2.6 copy-start.13
  86.7 2.6 copy-start.15
  94.5 3.2 copy-start.14
  94.5 3.2 copy-start.16
  97.7 2.6 copy-start.13
  97.7 2.6 copy-start.15
  105.5 3.1 copy-start.14
  105.5 3.1 copy-start.16
  108.6 22.1 %copy-start.8 = (bf16[2,1,1,128,1024]{4,3,2,1,0:T(8,128)(2,1)S(1)}, bf16[2,1,1,128,1024]{4,3,2,1,0:T(8,128)(2,1)}, u32[]{:S(2)}) copy-start(bf16[2,1,1,128,1024]{4,3,2,1,0:T(8,128)(2,1)} %param.11) | copy-start | bytes 1572868
  111.6 17.5 %collective-permute-start = (bf16[128,1024]{1,0:T(8,128)(2,1)S(1)}, bf16[128,1024]{1,0:T(8,128)(2,1)S(1)}, u32[]{:S(2)}, u32[]{:S(2)}) collective-permute-start(bf16[128,1024]{1,0:T(8,128)(2,1)S(1)} %fusion.63), channel_id=1, source_target_pairs={{448,0},{0,64},{64,128},{128,192},{192,256},{256,320},{320,384},{3... | collective-permute-start | bytes 786440 | tf_op jit(solution)/shard_map/ppermute | solution.py:14
  129.1 18.6 %copy-start.2 = (bf16[128,1024]{1,0:T(8,128)(2,1)}, bf16[128,1024]{1,0:T(8,128)(2,1)S(1)}, u32[]{:S(2)}) copy-start(bf16[128,1024]{1,0:T(8,128)(2,1)S(1)} %collective-permute-done) | copy-start | bytes 786436
  129.3 0.6 copy-start.21
  129.6 4.4 copy-start.5
  129.9 0.9 copy-start.17
  130.6 143.5 %reduce-scatter.3.cloned.1.call-start = ((), (), s32[]{:S(2)}) async-start(), calls=%async_computation.4 | async-start | bytes 1114112 | tf_op jit(solution)/shard_map/reduce_scatter | solution.py:124
  147.1 203.9 %reduce-scatter.5.cloned.1.call-start = ((), (), s32[]{:S(2)}) async-start(), calls=%async_computation.5 | async-start | bytes 1114112 | tf_op jit(solution)/shard_map/reduce_scatter | solution.py:124
  201.6 2.6 copy-start.9
  201.6 2.6 copy-start.11
  209.5 3.2 copy-start.10
  209.5 3.2 copy-start.12
  212.6 2.6 copy-start.9
  212.6 2.6 copy-start.11
  220.5 3.1 copy-start.10
  220.5 3.1 copy-start.12
  223.6 3.8 copy-start.4
  223.6 6.1 %copy-start.7 = (bf16[2048,256]{1,0:T(8,128)(2,1)S(1)}, bf16[2048,256]{1,0:T(8,128)(2,1)}, u32[]{:S(2)}) copy-start(bf16[2048,256]{1,0:T(8,128)(2,1)} %all-gather.5.cloned.1.call-done) | copy-start | bytes 3145732
  233.6 43.1 %copy-start.20 = (f32[128]{0:T(128)S(1)}, f32[128]{0:T(128)}, u32[]{:S(2)}) copy-start(f32[128]{0:T(128)} %copy-done.19) | copy-start | bytes 1540
  237.6 113.4 %copy-start.6 = (f32[128,256]{1,0:T(8,128)S(1)}, f32[128,256]{1,0:T(8,128)}, u32[]{:S(2)}) copy-start(f32[128,256]{1,0:T(8,128)} %copy-done.5) | copy-start | bytes 393220
  237.6 113.4 %copy-start.18 = (f32[128]{0:T(128)S(1)}, f32[128]{0:T(128)}, u32[]{:S(2)}) copy-start(f32[128]{0:T(128)} %copy-done.17) | copy-start | bytes 1540
  237.6 116.0 %copy-start.3 = (bf16[128,1024]{1,0:T(8,128)(2,1)S(1)}, bf16[128,1024]{1,0:T(8,128)(2,1)}, u32[]{:S(2)}) copy-start(bf16[128,1024]{1,0:T(8,128)(2,1)} %copy-done.2) | copy-start | bytes 786436
  237.6 116.0 %copy-start.22 = (f32[128]{0:T(128)S(1)}, f32[128]{0:T(128)}, u32[]{:S(2)}) copy-start(f32[128]{0:T(128)} %copy-done.21) | copy-start | bytes 1540
  239.8 273.3 %all-reduce.3.cloned.1.call-start = ((), (), s32[]{:S(2)}) async-start(), calls=%async_computation.6 | async-start | bytes 4194304 | tf_op jit(solution)/shard_map/psum | solution.py:145
  355.7 235.8 %all-reduce.5.cloned.1.call-start = ((), (), s32[]{:S(2)}) async-start(), calls=%async_computation.7 | async-start | bytes 4194304 | tf_op jit(solution)/shard_map/psum | solution.py:145
  516.1 19.7 %collective-permute-start.1 = (bf16[128,1024]{1,0:T(8,128)(2,1)S(1)}, bf16[128,1024]{1,0:T(8,128)(2,1)S(1)}, u32[]{:S(2)}, u32[]{:S(2)}) collective-permute-start(bf16[128,1024]{1,0:T(8,128)(2,1)S(1)} %add_convert_fusion), channel_id=1, source_target_pairs={{448,0},{0,64},{64,128},{128,192},{192,256},{256,320},{320,384},{3... | collective-permute-start | bytes 786440 | tf_op jit(solution)/shard_map/ppermute | solution.py:14
Sparse Core Ops, SparseCore 0:
  12.8 69.2 all-gather.2
  130.8 66.2 all-gather.4
  199.9 74.2 reduce-scatter.2
  277.6 73.3 reduce-scatter.4
  355.8 157.2 all-reduce.2
  515.4 76.0 all-reduce.4
